TPU v7x, 32 devices: a whole 2x2x4 slice. The times are simulated.
32 devices in a mesh: parts: 2 (over y), rows: 4 (over x, core), cols: 4 (over z).
Axes of the slice: x: 2, y: 2, z: 4, core: 2. Of those that a mesh axis runs over, the one named last changes fastest.
Arguments:
- pair: float32 [256, 4, 32, 128], P(('parts', 'rows'), None, 'cols'), parts along dimension 0, may hold values from -6 to 6
- singles: float32 [256, 384], P(('parts', 'rows')), parts along dimension 0, may hold values from -6 to 6
- restype: int32 [256], P(('parts', 'rows')), parts along dimension 0, may hold values from 0 to 31
- block_mask: int32 [32, 4, 4], P(('parts', 'rows'), None, 'cols'), parts along dimension 0, may hold values from 0 to 1, as said below
- ln_trans: float32 [128], replicated, may hold values from 0.1 to 1.9
- w_trans_in: bfloat16 [128, 1024], replicated, may hold values from -0.5 to 0.5
- w_trans_out: bfloat16 [512, 128], replicated, may hold values from -0.25 to 0.25
- ln_bias: float32 [128], replicated, may hold values from 0.1 to 1.9
- w_bias: bfloat16 [128, 16], replicated, may hold values from -0.5 to 0.5
- restype_table: float32 [32, 384], replicated, may hold values from -6 to 6
- ln_single: float32 [384], replicated, may hold values from 0.1 to 1.9
- w_attn: bfloat16 [384, 1536], replicated, may hold values from -80 to 80
- w_single_out: bfloat16 [384, 384], replicated, may hold values from -0.3125 to 0.3125
- w_dist: bfloat16 [128, 64], replicated, may hold values from -0.5 to 0.5
- dist_bias: float32 [64], replicated, may hold values from -6 to 6
Outputs:
- pair_next: float32 [256, 4, 32, 128], P(('parts', 'rows'), None, 'cols'), parts along dimension 0
- singles_next: float32 [256, 384], P(('parts', 'rows')), parts along dimension 0
- dist_logits: float32 [256, 4, 2048], P(('parts', 'rows'), None, 'cols'), parts along dimension 0
There are 2 independent parts, one for each index of `parts`. A program takes and returns all parts, laid end to end along the dimension named above; an argument that names none is the same for every part. Nothing has to cross between parts.
Inputs may be any that keep to these rules, and one draw needn't show every extreme that they name: block_mask[p, a, c] is 1 where p == a * 4 + c.
All inputs are finite; a program needn't handle non-finite values.
Results may differ from a plain program's by a relative error of at most 0.0044.
Values may be sent and summed in bfloat16 or wider, within the bound.
No kernel may reach another device: no remote copies, remote signals or barrier semaphores. Data moves between devices by JAX's collectives and lax.ppermute only.
A program may use at most 64 MiB of HBM per device.

v0:
```python
import math
import jax
import jax.numpy as jnp
from jax import lax
from jax.sharding import PartitionSpec as P

eps_norm = 1e-05


def layer_norm(values, gain_vec):
    average = jnp.mean(values, axis=-1, keepdims=True)
    centred = values - average
    spread = jnp.mean(centred * centred, axis=-1, keepdims=True)
    return centred * lax.rsqrt(spread + eps_norm) * gain_vec


def pair_block(pair_rows, ln_trans, w_trans_in, w_trans_out, ln_bias, w_bias, w_dist):
    hidden_units = w_trans_out.shape[0]
    normed = layer_norm(pair_rows, ln_trans).astype(jnp.bfloat16)
    gate_up = jnp.dot(normed, w_trans_in, preferred_element_type=jnp.float32)
    hidden = (jax.nn.silu(gate_up[:, :hidden_units]) * gate_up[:, hidden_units:]).astype(
        jnp.bfloat16
    )
    updated = pair_rows + jnp.dot(hidden, w_trans_out, preferred_element_type=jnp.float32)
    biased = layer_norm(updated, ln_bias).astype(jnp.bfloat16)
    head_bias = jnp.dot(biased, w_bias, preferred_element_type=jnp.float32)
    binned = jnp.dot(
        updated.astype(jnp.bfloat16), w_dist, preferred_element_type=jnp.float32
    ).astype(jnp.bfloat16)
    return (updated, head_bias, binned)


def local(
    pair,
    singles,
    restype,
    block_mask,
    ln_trans,
    w_trans_in,
    w_trans_out,
    ln_bias,
    w_bias,
    restype_table,
    ln_single,
    w_attn,
    w_single_out,
    w_dist,
    dist_bias,
):
    queries, key_groups, block_len, channels = pair.shape
    key_count = key_groups * block_len
    q_groups = queries // block_len
    head_count = w_bias.shape[1]
    model_width = w_single_out.shape[0]
    head_width = model_width // head_count
    bin_count = w_dist.shape[1]
    step_rows = math.gcd(queries, 16)
    pair_tiles = pair.reshape(queries // step_rows, step_rows * key_count, channels)

    def run_tile(pair_tile):
        return pair_block(pair_tile, ln_trans, w_trans_in, w_trans_out, ln_bias, w_bias, w_dist)

    updated, head_bias, binned = lax.map(run_tile, pair_tiles)
    pair_next = updated.reshape(queries, key_groups, block_len, channels)
    head_bias = head_bias.reshape(queries, key_count, head_count)
    binned = binned.reshape(queries, key_groups, block_len, bin_count)
    type_count = restype_table.shape[0]
    one_hot = (restype[:, None] == jnp.arange(type_count, dtype=jnp.int32)[None, :]).astype(
        jnp.float32
    )
    embedded = singles + jnp.dot(one_hot, restype_table, precision=lax.Precision.HIGHEST)
    normed_s = layer_norm(embedded, ln_single).astype(jnp.bfloat16)
    query_proj = (
        jnp.dot(normed_s, w_attn[:, :model_width], preferred_element_type=jnp.float32)
        * head_width ** (-0.5)
    ).astype(jnp.bfloat16)
    gate_vals = jax.nn.sigmoid(
        jnp.dot(normed_s, w_attn[:, 3 * model_width :], preferred_element_type=jnp.float32)
    )
    key_weights = w_attn[:, model_width : 3 * model_width]
    own_rows = lax.dynamic_slice_in_dim(normed_s, lax.axis_index("cols") * block_len, block_len, 0)
    local_kv = jnp.dot(own_rows, key_weights, preferred_element_type=jnp.float32).astype(
        jnp.bfloat16
    )
    key_values = lax.all_gather(local_kv, "rows", axis=0, tiled=True)
    q_heads = query_proj.reshape(queries, head_count, head_width)
    k_heads = key_values[:, :model_width].reshape(key_count, head_count, head_width)
    v_heads = key_values[:, model_width:].reshape(key_count, head_count, head_width)
    scores = jnp.einsum("qhd,khd->hqk", q_heads, k_heads, preferred_element_type=jnp.float32)
    scores = scores + jnp.transpose(head_bias, (2, 0, 1))
    allowed = (
        jnp.broadcast_to(
            block_mask[:, None, :, :], (q_groups, block_len, key_groups, block_len)
        ).reshape(queries, key_count)
        > 0
    )
    scores = jnp.where(allowed[None], scores, jnp.float32(-1000000000.0))
    local_max = jnp.max(scores, axis=-1)
    row_max = lax.pmax(local_max, "cols")
    expo = jnp.exp(scores - row_max[:, :, None])
    totals = jnp.sum(expo, axis=-1)
    weighted = jnp.einsum(
        "hqk,khd->qhd", expo.astype(jnp.bfloat16), v_heads, preferred_element_type=jnp.float32
    ).reshape(queries, model_width)
    totals, weighted = (
        lax.psum(totals.astype(jnp.bfloat16), "cols").astype(jnp.float32),
        lax.psum(weighted.astype(jnp.bfloat16), "cols").astype(jnp.float32),
    )
    normalised = (
        weighted.reshape(queries, head_count, head_width) / jnp.transpose(totals)[:, :, None]
    )
    attended = (gate_vals * normalised.reshape(queries, model_width)).astype(jnp.bfloat16)
    singles_next = embedded + jnp.dot(attended, w_single_out, preferred_element_type=jnp.float32)
    grouped = binned.reshape(q_groups, block_len, key_groups, block_len * bin_count)
    outgoing = jnp.transpose(grouped, (2, 0, 1, 3)).reshape(
        key_groups * q_groups, 1, block_len, block_len * bin_count
    )
    arrived = lax.all_to_all(outgoing, ("rows", "cols"), split_axis=0, concat_axis=1, tiled=True)
    mirrored = jnp.transpose(
        arrived.reshape(key_groups, q_groups, block_len, block_len, bin_count), (1, 3, 0, 2, 4)
    )
    mirrored = mirrored.reshape(queries, key_groups, block_len, bin_count)
    logits = binned.astype(jnp.float32) + mirrored.astype(jnp.float32) + dist_bias
    dist_logits = logits.reshape(queries, key_groups, block_len * bin_count)
    return (pair_next, singles_next, dist_logits)


def solution(mesh):
    return jax.shard_map(
        local,
        mesh=mesh,
        in_specs=(
            P(("parts", "rows"), None, "cols", None),
            P(("parts", "rows"), None),
            P(("parts", "rows")),
            P(("parts", "rows"), None, "cols"),
            P(),
            P(),
            P(),
            P(),
            P(),
            P(),
            P(),
            P(),
            P(),
            P(),
            P(),
        ),
        out_specs=(
            P(("parts", "rows"), None, "cols", None),
            P(("parts", "rows"), None),
            P(("parts", "rows"), None, "cols"),
        ),
        check_vma=False,
    )
```

profile of v0, /device:TPU:0, one launch (start us, length us, event | category | flops | bytes accessed | tf_op | source)
XLA Modules:
  0.0 56.2 jit_solution(419873935561623359)
XLA Ops:
  0.7 8.1 %while.14 = (s32[]{:T(128)}, f32[2,512,128]{2,1,0:T(8,128)S(1)}, f32[2,512,16]{1,0,2:T(2,128)S(1)}, bf16[2,512,64]{1,2,0:T(8,128)(2,1)S(1)}, f32[2,512,128]{2,1,...) while((s32[]{:T(128)}, f32[2,512,128]{2,1,0:T(8,128)S(1)}, ...), condition=%wide.region_5.6_spmd, body=%wide.region_0.5_spmd.sunk | while | flops 214598656 | bytes 10466621 | solution.py:63
  0.7 1.1 %fusion.65 = (f32[512]{0:T(512)S(1)}, f32[1,512,128]{2,1,0:T(8,128)S(1)}) fusion(f32[2,512,128]{2,1,0:T(8,128)} %get-tuple-element.248, s32[]{:T(128)S(6)} %copy.112), kind=kLoop, calls=%fused_computation.63.clone.1 | loop fusion | flops 65024 | bytes 526340 | tf_op jit(solution)/shard_map/while/body/eval_jaxpr/reduce_sum | solution.py:11
  2.1 0.5 fusion.66
  2.6 0.4 copy-done.14
  3.0 0.5 fusion.67
  3.7 0.4 copy-done.4
  4.1 0.2 convolution_bitcast_fusion.2
  4.8 1.1 %fusion.65 = (f32[512]{0:T(512)S(1)}, f32[1,512,128]{2,1,0:T(8,128)S(1)}) fusion(f32[2,512,128]{2,1,0:T(8,128)} %get-tuple-element.248, s32[]{:T(128)S(6)} %copy.112), kind=kLoop, calls=%fused_computation.63.clone.1 | loop fusion | flops 65024 | bytes 526340 | tf_op jit(solution)/shard_map/while/body/eval_jaxpr/reduce_sum | solution.py:11
  6.2 0.5 fusion.66
  6.7 0.4 copy-done.14
  7.0 0.5 fusion.67
  7.8 0.4 copy-done.4
  8.2 0.2 convolution_bitcast_fusion.2
  9.2 0.7 %copy.81 = bf16[4,4,8,512]{3,2,1,0:T(8,128)(2,1)} copy(bf16[4,4,8,512]{3,0,2,1:T(4,128)(2,1)S(1)} %bitcast.74) | data formatting | bytes 262144 | tf_op jit(solution)/shard_map/transpose | solution.py:115
  9.9 7.4 %all-to-all-start = ((bf16[16,1,8,512]{3,2,1,0:T(8,128)(2,1)}), bf16[16,1,8,512]{3,2,1,0:T(8,128)(2,1)S(1)}, u32[]{:S(2)}, u32[]{:S(2)}) async-start(bf16[16,1,8,512]{3,2,1,0:T(8,128)(2,1)} %bitcast.16), calls=%async_computation | async-start | bytes 262144 | tf_op jit(solution)/shard_map/all_to_all | solution.py:118
  17.3 0.3 fusion.38
  18.7 5.3 %all_gather.3 = bf16[32,768]{1,0:T(8,128)(2,1)S(1)} all-gather(bf16[8,768]{1,0:T(8,128)(2,1)S(1)} %convolution_convert_fusion.2), channel_id=1, replica_groups=mesh['parts'=2,'rows'=4,'cols'=4] {'rows'}, dimensions={0}, use_global_device_ids=true | all-gather | bytes 61440 | tf_op jit(solution)/shard_map/all_gather | solution.py:85
  24.5 0.3 fusion.39
  24.8 12.1 %pmax.7 = f32[16,32]{1,0:T(8,128)S(1)} all-reduce(f32[16,32]{1,0:T(8,128)S(1)} %get-tuple-element.141), channel_id=1, replica_groups=mesh['parts'=2,'rows'=4,'cols'=4] {'cols'}, use_global_device_ids=true, to_apply=%region_9.10 | all-reduce | flops 512 | bytes 4096 | tf_op jit(solution)/shard_map/pmax | solution.py:99
  37.0 0.2 convolution_convert_fusion.1
  37.6 15.8 %all-reduce = (bf16[32,16]{0,1:T(8,128)(2,1)S(1)}, bf16[32,384]{1,0:T(8,128)(2,1)S(1)}) all-reduce(bf16[32,16]{0,1:T(8,128)(2,1)S(1)} %bitcast.79, bf16[32,384]{1,0:T(8,128)(2,1)S(1)} %copy.89), channel_id=1, replica_groups=mesh['parts'=2,'rows'=4,'cols'=4] {'cols'}, use_global_device_ids=true, to_apply=%region_12.13 | all-reduce | flops 12800 | bytes 51200 | tf_op jit(solution)/shard_map/psum | solution.py:106
  53.7 0.2 reshape.110
  54.0 1.0 %convolution_add_fusion.3 = f32[32,384]{1,0:T(8,128)} fusion(f32[32,384]{1,0:T(8,128)S(1)} %get-tuple-element.140, bf16[384,384]{1,0:T(8,128)(2,1)S(1)} %copy-done, bf16[32,384]{1,0:T(8,128)(2,1)S(1)} %multiply_convert_fusion.4, bf16[384,1536]{1,0:T(8,128)(2,1)S(1)} %copy-done.2, f32[32,384]{1,0:T(8,128)S(1)} %div.40, ...), kind=kOutput, calls=%fused_computation.36 | convolution fusion | flops 18972672 | bytes 786432 | tf_op jit(solution)/shard_map/dot_general | solution.py:113
  55.4 0.8 %add_add_fusion = f32[32,4,512]{2,1,0:T(4,128)} fusion(f32[32,4,512]{2,1,0:T(4,128)S(1)} %reshape.110, f32[32,4,512]{2,1,0:T(4,128)S(1)} %reshape.111, f32[512]{0:T(512)S(1)} %add.82), kind=kLoop, calls=%fused_computation.44 | loop fusion | flops 131072 | bytes 788480 | tf_op jit(solution)/shard_map/add | solution.py:123
  (95 shorter events, 4.7 us)
Async XLA Ops:
  0.6 53.4 %copy-start = (bf16[384,384]{1,0:T(8,128)(2,1)S(1)}, bf16[384,384]{1,0:T(8,128)(2,1)}, u32[]{:S(2)}) copy-start(bf16[384,384]{1,0:T(8,128)(2,1)} %param.29) | copy-start | bytes 884740
  0.7 1.4 %copy-start.1 = (bf16[128,1024]{1,0:T(8,128)(2,1)S(1)}, bf16[128,1024]{1,0:T(8,128)(2,1)}, u32[]{:S(2)}) copy-start(bf16[128,1024]{1,0:T(8,128)(2,1)} %get-tuple-element.250) | copy-start | bytes 786436 | tf_op jit(solution)/shard_map/while
  0.7 1.4 %copy-start.8 = (f32[128]{0:T(128)S(1)}, f32[128]{0:T(128)}, u32[]{:S(2)}) copy-start(f32[128]{0:T(128)} %get-tuple-element.249) | copy-start | bytes 1540 | tf_op jit(solution)/shard_map/while
  2.1 0.9 %copy-start.14 = (bf16[512,128]{1,0:T(8,128)(2,1)S(1)}, bf16[512,128]{1,0:T(8,128)(2,1)}, u32[]{:S(2)}) copy-start(bf16[512,128]{1,0:T(8,128)(2,1)} %get-tuple-element.251) | copy-start | bytes 393220 | tf_op jit(solution)/shard_map/while
  3.5 0.7 %copy-start.4 = (bf16[128,16]{0,1:T(8,128)(2,1)S(1)}, bf16[128,16]{0,1:T(8,128)(2,1)}, u32[]{:S(2)}) copy-start(bf16[128,16]{0,1:T(8,128)(2,1)} %get-tuple-element.253) | copy-start | bytes 12292 | tf_op jit(solution)/shard_map/while
  3.5 0.7 %copy-start.7 = (f32[128]{0:T(128)S(1)}, f32[128]{0:T(128)}, u32[]{:S(2)}) copy-start(f32[128]{0:T(128)} %get-tuple-element.252) | copy-start | bytes 1540 | tf_op jit(solution)/shard_map/while
  3.5 1.1 %copy-start.3 = (bf16[128,64]{0,1:T(8,128)(2,1)S(1)}, bf16[128,64]{0,1:T(8,128)(2,1)}, u32[]{:S(2)}) copy-start(bf16[128,64]{0,1:T(8,128)(2,1)} %get-tuple-element.254) | copy-start | bytes 49156 | tf_op jit(solution)/shard_map/while
  4.7 1.4 %copy-start.1 = (bf16[128,1024]{1,0:T(8,128)(2,1)S(1)}, bf16[128,1024]{1,0:T(8,128)(2,1)}, u32[]{:S(2)}) copy-start(bf16[128,1024]{1,0:T(8,128)(2,1)} %get-tuple-element.250) | copy-start | bytes 786436 | tf_op jit(solution)/shard_map/while
  4.8 1.4 %copy-start.8 = (f32[128]{0:T(128)S(1)}, f32[128]{0:T(128)}, u32[]{:S(2)}) copy-start(f32[128]{0:T(128)} %get-tuple-element.249) | copy-start | bytes 1540 | tf_op jit(solution)/shard_map/while
  6.1 0.9 %copy-start.14 = (bf16[512,128]{1,0:T(8,128)(2,1)S(1)}, bf16[512,128]{1,0:T(8,128)(2,1)}, u32[]{:S(2)}) copy-start(bf16[512,128]{1,0:T(8,128)(2,1)} %get-tuple-element.251) | copy-start | bytes 393220 | tf_op jit(solution)/shard_map/while
  7.5 0.7 %copy-start.4 = (bf16[128,16]{0,1:T(8,128)(2,1)S(1)}, bf16[128,16]{0,1:T(8,128)(2,1)}, u32[]{:S(2)}) copy-start(bf16[128,16]{0,1:T(8,128)(2,1)} %get-tuple-element.253) | copy-start | bytes 12292 | tf_op jit(solution)/shard_map/while
  7.5 0.7 %copy-start.7 = (f32[128]{0:T(128)S(1)}, f32[128]{0:T(128)}, u32[]{:S(2)}) copy-start(f32[128]{0:T(128)} %get-tuple-element.252) | copy-start | bytes 1540 | tf_op jit(solution)/shard_map/while
  7.5 1.1 %copy-start.3 = (bf16[128,64]{0,1:T(8,128)(2,1)S(1)}, bf16[128,64]{0,1:T(8,128)(2,1)}, u32[]{:S(2)}) copy-start(bf16[128,64]{0,1:T(8,128)(2,1)} %get-tuple-element.254) | copy-start | bytes 49156 | tf_op jit(solution)/shard_map/while
  8.8 9.4 %copy-start.13 = (f32[2,512,128]{2,1,0:T(8,128)}, f32[2,512,128]{2,1,0:T(8,128)S(1)}, u32[]{:S(2)}) copy-start(f32[2,512,128]{2,1,0:T(8,128)S(1)} %get-tuple-element.62) | copy-start | bytes 1572868
  8.8 8.5 %copy-start.5 = (f32[32,384]{1,0:T(8,128)S(1)}, f32[32,384]{1,0:T(8,128)}, u32[]{:S(2)}) copy-start(f32[32,384]{1,0:T(8,128)} %param.18) | copy-start | bytes 147460
  8.8 8.5 %copy-start.6 = (f32[32,384]{1,0:T(8,128)S(1)}, f32[32,384]{1,0:T(8,128)}, u32[]{:S(2)}) copy-start(f32[32,384]{1,0:T(8,128)} %param.26) | copy-start | bytes 147460
  8.8 8.5 %copy-start.11 = (s32[32]{0:T(128)S(1)}, s32[32]{0:T(128)}, u32[]{:S(2)}) copy-start(s32[32]{0:T(128)} %param.19) | copy-start | bytes 388
  8.8 9.3 %copy-start.9 = (f32[384]{0:T(512)S(1)}, f32[384]{0:T(512)}, u32[]{:S(2)}) copy-start(f32[384]{0:T(512)} %param.27) | copy-start | bytes 4612
  8.8 9.4 %copy-start.2 = (bf16[384,1536]{1,0:T(8,128)(2,1)S(1)}, bf16[384,1536]{1,0:T(8,128)(2,1)}, u32[]{:S(2)}) copy-start(bf16[384,1536]{1,0:T(8,128)(2,1)} %param.28) | copy-start | bytes 3538948
  9.9 45.1 %all-to-all-start = ((bf16[16,1,8,512]{3,2,1,0:T(8,128)(2,1)}), bf16[16,1,8,512]{3,2,1,0:T(8,128)(2,1)S(1)}, u32[]{:S(2)}, u32[]{:S(2)}) async-start(bf16[16,1,8,512]{3,2,1,0:T(8,128)(2,1)} %bitcast.16), calls=%async_computation | async-start | bytes 262144 | tf_op jit(solution)/shard_map/all_to_all | solution.py:118
  17.6 6.6 %copy-start.10 = (s32[4,4,1]{1,2,0:T(1,128)S(1)}, s32[4,4,1]{1,2,0:T(1,128)}, u32[]{:S(2)}) copy-start(s32[4,4,1]{1,2,0:T(1,128)} %param.20) | copy-start | bytes 196
  37.3 16.7 %copy-start.12 = (f32[64]{0:T(128)S(1)}, f32[64]{0:T(128)}, u32[]{:S(2)}) copy-start(f32[64]{0:T(128)} %param.31) | copy-start | bytes 772
where the time goes:
time: 56.6 us; the launch traced here: 56.2 us
  blocking collectives  33.3 us (59%)
  starting transfers between devices  7.39 us (13%)
  local copies, waits for them, and re-layouts  5.89 us (10%)
  matrix products  4.73 us (8%)
  other arithmetic  3.66 us (6%)
  between operations  0.96 us (2%)
    psum x1, blocking collectives, local(): lax.psum(totals.astype(jnp.bfloat16), 'cols').astype(jnp.float32)  15.8 us
    pmax x1, blocking collectives, local(): row_max = lax.pmax(local_max, 'cols')  12.1 us
    all_to_all x1, starting transfers between devices, local(): lax.all_to_all(outgoing, ('rows', 'cols'), split_axis=0, concat_axis=1, t...  7.39 us
    all_gather x1, blocking collectives, local(): key_values = lax.all_gather(local_kv, 'rows', axis=0, tiled=True)  5.33 us
    reduce_sum x2, other arithmetic, layer_norm(): average = jnp.mean(values, axis=-1, keepdims=True)  2.28 us
    while x24, local copies, waits for them, and re-layouts  1.65 us
  transfers between devices with their start and end apart: 1, of which 0 were waited for; matrix products, arithmetic and copies ran while one was open for 7% of the time, Pallas kernels for 0%

commit v1 on v0

--- a/solution.py
+++ b/solution.py
@@ -5,6 +5,18 @@
 from jax.sharding import PartitionSpec as P
 
 eps_norm = 1e-05
+
+
+def in_blocks(value, dim, count):
+    shape = value.shape
+    parts = value.reshape(*shape[:dim], count, shape[dim] // count, *shape[dim + 1 :])
+    return jnp.moveaxis(parts, dim, 0)
+
+
+def laid_out(tiles, dim):
+    shape = list(tiles.shape[1:])
+    shape[dim] *= tiles.shape[0]
+    return jnp.moveaxis(tiles, 0, dim).reshape(shape)
 
 
 def layer_norm(values, gain_vec):
@@ -115,7 +127,17 @@
     outgoing = jnp.transpose(grouped, (2, 0, 1, 3)).reshape(
         key_groups * q_groups, 1, block_len, block_len * bin_count
     )
-    arrived = lax.all_to_all(outgoing, ("rows", "cols"), split_axis=0, concat_axis=1, tiled=True)
+    length, position = (lax.axis_size(("rows", "cols")), lax.axis_index(("rows", "cols")))
+    blocks = in_blocks(outgoing, 0, length)
+    out = blocks
+    for hop in range(1, length):
+        target, source = ((position + hop) % length, (position - hop) % length)
+        sent = lax.dynamic_index_in_dim(blocks, target, 0)
+        partner_block = lax.ppermute(
+            sent, ("rows", "cols"), [(i, (i + hop) % length) for i in range(length)]
+        )
+        out = lax.dynamic_update_slice_in_dim(out, partner_block, source, axis=0)
+    arrived = laid_out(out, 1)
     mirrored = jnp.transpose(
         arrived.reshape(key_groups, q_groups, block_len, block_len, bin_count), (1, 3, 0, 2, 4)
     )

time: 56.6 us -> 73 us (1.29)
  starting transfers between devices: 7.39 us -> 21.9 us
  waiting for transfers between devices: 0.01 us -> 2.11 us
    ppermute x0 -> x15, starting transfers between devices: none -> 21.9 us  [local(): lax.ppermute(sent, ('rows', 'cols'), [(i, (i + hop) % length) for i in ra...]
    all_to_all x1 -> x0, starting transfers between devices: 7.39 us -> none  [local(): lax.all_to_all(outgoing, ('rows', 'cols'), split_axis=0, concat_axis=1, t...]
    ppermute x0 -> x15, waiting for transfers between devices: none -> 2.11 us  [local(): lax.ppermute(sent, ('rows', 'cols'), [(i, (i + hop) % length) for i in ra...]
    psum x1, blocking collectives: 15.8 us -> 17.5 us  [local(): lax.psum(weighted.astype(jnp.bfloat16), 'cols').astype(jnp.float32)]
    pmax x1, blocking collectives: 12.1 us -> 10.6 us  [local(): row_max = lax.pmax(local_max, 'cols')]
    dynamic_update_slice x8, local copies, waits for them, and re-layouts: 0.69 us -> 2.09 us  [local(): updated, head_bias, binned = lax.map(run_tile, pair_tiles)]
    while x24, local copies, waits for them, and re-layouts: 1.65 us -> 0.81 us
  transfers between devices with their start and end apart: 1 -> 15, of which waited for: 0 -> 2; matrix products, arithmetic and copies ran while one was open for 7% -> 5% of each run, Pallas kernels for 0% -> 0%
where the time goes in v1:
time: 73 us; the launch traced here: 72.7 us
  blocking collectives  33.3 us (46%)
  starting transfers between devices  21.9 us (30%)
  local copies, waits for them, and re-layouts  5.4 us (7%)
  matrix products  4.9 us (7%)
  other arithmetic  3.69 us (5%)
  waiting for transfers between devices  2.11 us (3%)
  between operations  1.17 us (2%)
    ppermute x15, starting transfers between devices, local(): lax.ppermute(sent, ('rows', 'cols'), [(i, (i + hop) % length) for i in ra...  21.9 us
    psum x1, blocking collectives, local(): lax.psum(weighted.astype(jnp.bfloat16), 'cols').astype(jnp.float32)  17.5 us
    pmax x1, blocking collectives, local(): row_max = lax.pmax(local_max, 'cols')  10.6 us
    all_gather x1, blocking collectives, local(): key_values = lax.all_gather(local_kv, 'rows', axis=0, tiled=True)  5.24 us
    reduce_sum x2, other arithmetic, layer_norm(): average = jnp.mean(values, axis=-1, keepdims=True)  2.28 us
    ppermute x15, waiting for transfers between devices, local(): lax.ppermute(sent, ('rows', 'cols'), [(i, (i + hop) % length) for i in ra...  2.11 us
    dynamic_update_slice x8, local copies, waits for them, and re-layouts, local(): updated, head_bias, binned = lax.map(run_tile, pair_tiles)  2.09 us
  transfers between devices with their start and end apart: 15, of which 2 were waited for; matrix products, arithmetic and copies ran while one was open for 5% of the time, Pallas kernels for 0%

profile of v1, /device:TPU:0, one launch (start us, length us, event | category | flops | bytes accessed | tf_op | source)
XLA Modules:
  0.0 72.7 jit_solution(141157663400018448)
XLA Ops:
  0.7 8.7 %while.14 = (s32[]{:T(128)}, f32[2,512,128]{2,1,0:T(8,128)}, f32[2,512,16]{1,0,2:T(2,128)S(1)}, bf16[2,512,64]{1,2,0:T(8,128)(2,1)S(1)}, f32[2,512,128]{2,1,0:T(...) while((s32[]{:T(128)}, f32[2,512,128]{2,1,0:T(8,128)}, ...), condition=%wide.region_5.6_spmd, body=%wide.region_0.5_spmd.sunk | while | flops 214598656 | bytes 10466621 | solution.py:75
  0.7 1.1 %fusion.63 = (f32[512]{0:T(512)S(1)}, f32[1,512,128]{2,1,0:T(8,128)S(1)}) fusion(f32[2,512,128]{2,1,0:T(8,128)} %get-tuple-element.230, s32[]{:T(128)S(6)} %copy.65), kind=kLoop, calls=%fused_computation.92.clone.1 | loop fusion | flops 65024 | bytes 526340 | tf_op jit(solution)/shard_map/while/body/eval_jaxpr/reduce_sum | solution.py:23
  3.6 0.7 constant_dynamic-update-slice_fusion.17
  5.1 1.1 %fusion.63 = (f32[512]{0:T(512)S(1)}, f32[1,512,128]{2,1,0:T(8,128)S(1)}) fusion(f32[2,512,128]{2,1,0:T(8,128)} %get-tuple-element.230, s32[]{:T(128)S(6)} %copy.65), kind=kLoop, calls=%fused_computation.92.clone.1 | loop fusion | flops 65024 | bytes 526340 | tf_op jit(solution)/shard_map/while/body/eval_jaxpr/reduce_sum | solution.py:23
  8.0 0.7 constant_dynamic-update-slice_fusion.17
  9.8 3.1 %collective-permute-start = (bf16[1,1,1,8,512]{4,3,0,2,1:T(8,128)(2,1)S(1)}, bf16[1,1,1,8,512]{4,3,0,2,1:T(8,128)(2,1)S(1)}, u32[]{:S(2)}, u32[]{:S(2)}) collective-permute-start(bf16[1,1,1,8,512]{4,3,0,2,1:T(8,128)(2,1)S(1)} %constant_dynamic-slice_fusion.15), channel_id=1, source_target_pairs={{0,1},{1,2},{2,3},{3,4},{4,5},{5,6},{6,7},{7,8},{8,9},{9,10},{10,1... | collective-permute-start | bytes 24584 | tf_op jit(solution)/shard_map/ppermute | solution.py:136
  14.2 5.2 %all_gather.3 = bf16[32,768]{1,0:T(8,128)(2,1)S(1)} all-gather(bf16[8,768]{1,0:T(8,128)(2,1)S(1)} %convolution_convert_fusion.2), channel_id=1, replica_groups=mesh['parts'=2,'rows'=4,'cols'=4] {'rows'}, dimensions={0}, use_global_device_ids=true | all-gather | bytes 61440 | tf_op jit(solution)/shard_map/all_gather | solution.py:97
  20.7 10.6 %pmax.7 = f32[16,32]{1,0:T(8,128)S(1)} all-reduce(f32[16,32]{1,0:T(8,128)S(1)} %get-tuple-element.123), channel_id=1, replica_groups=mesh['parts'=2,'rows'=4,'cols'=4] {'cols'}, use_global_device_ids=true, to_apply=%region_9.10 | all-reduce | flops 512 | bytes 4096 | tf_op jit(solution)/shard_map/pmax | solution.py:111
  31.6 17.5 %all-reduce = (bf16[32,384]{0,1:T(8,128)(2,1)S(1)}, bf16[32,16]{0,1:T(8,128)(2,1)S(1)}) all-reduce(bf16[32,384]{0,1:T(8,128)(2,1)S(1)} %bitcast.80, bf16[32,16]{0,1:T(8,128)(2,1)S(1)} %bitcast.83), channel_id=1, replica_groups=mesh['parts'=2,'rows'=4,'cols'=4] {'cols'}, use_global_device_ids=true, to_apply=%region_10.11 | all-reduce | flops 12800 | bytes 51200 | tf_op jit(solution)/shard_map/psum | solution.py:119
  49.1 1.1 %fusion.20 = f32[32,384]{1,0:T(8,128)} fusion(f32[32,384]{1,0:T(8,128)S(1)} %get-tuple-element.122, bf16[384,384]{1,0:T(8,128)(2,1)S(1)} %copy-done, f32[32,384]{0,1:T(8,128)S(1)} %bitcast_divide_fusion, bf16[32,384]{1,0:T(8,128)(2,1)S(1)} %multiply_convert_fusion.4, bf16[384,1536]{1,0:T(8,128)(2,1)S(1)} %copy-done.2), kind=kOutput, calls=%fused_computation.37 | convolution fusion | flops 18948096 | bytes 909312 | tf_op jit(solution)/shard_map/dot_general | solution.py:125
  50.3 0.7 %collective-permute-start.1 = (bf16[1,1,1,8,512]{4,3,0,2,1:T(8,128)(2,1)S(1)}, bf16[1,1,1,8,512]{4,3,0,2,1:T(8,128)(2,1)S(1)}, u32[]{:S(2)}, u32[]{:S(2)}) collective-permute-start(bf16[1,1,1,8,512]{4,3,0,2,1:T(8,128)(2,1)S(1)} %get-tuple-element.117), channel_id=1, source_target_pairs={{0,2},{1,3},{2,4},{3,5},{4,6},{5,7},{6,8},{7,9},{8,10},{9,11},{10,... | collective-permute-start | bytes 24584 | tf_op jit(solution)/shard_map/ppermute | solution.py:136
  51.3 1.5 %collective-permute-start.2 = (bf16[1,1,1,8,512]{4,3,0,2,1:T(8,128)(2,1)S(1)}, bf16[1,1,1,8,512]{4,3,0,2,1:T(8,128)(2,1)S(1)}, u32[]{:S(2)}, u32[]{:S(2)}) collective-permute-start(bf16[1,1,1,8,512]{4,3,0,2,1:T(8,128)(2,1)S(1)} %get-tuple-element.116), channel_id=1, source_target_pairs={{0,3},{1,4},{2,5},{3,6},{4,7},{5,8},{6,9},{7,10},{8,11},{9,12},{10... | collective-permute-start | bytes 24584 | tf_op jit(solution)/shard_map/ppermute | solution.py:136
  52.8 1.0 %collective-permute-start.3 = (bf16[1,1,1,8,512]{4,3,0,2,1:T(8,128)(2,1)S(1)}, bf16[1,1,1,8,512]{4,3,0,2,1:T(8,128)(2,1)S(1)}, u32[]{:S(2)}, u32[]{:S(2)}) collective-permute-start(bf16[1,1,1,8,512]{4,3,0,2,1:T(8,128)(2,1)S(1)} %get-tuple-element.115), channel_id=1, source_target_pairs={{0,4},{1,5},{2,6},{3,7},{4,8},{5,9},{6,10},{7,11},{8,12},{9,13},{1... | collective-permute-start | bytes 24584 | tf_op jit(solution)/shard_map/ppermute | solution.py:136
  53.8 0.6 collective-permute-start.4
  54.4 1.6 %collective-permute-start.5 = (bf16[1,1,1,8,512]{4,3,0,2,1:T(8,128)(2,1)S(1)}, bf16[1,1,1,8,512]{4,3,0,2,1:T(8,128)(2,1)S(1)}, u32[]{:S(2)}, u32[]{:S(2)}) collective-permute-start(bf16[1,1,1,8,512]{4,3,0,2,1:T(8,128)(2,1)S(1)} %get-tuple-element.113), channel_id=1, source_target_pairs={{0,6},{1,7},{2,8},{3,9},{4,10},{5,11},{6,12},{7,13},{8,14},{9,15},... | collective-permute-start | bytes 24584 | tf_op jit(solution)/shard_map/ppermute | solution.py:136
  56.0 2.9 %collective-permute-start.6 = (bf16[1,1,1,8,512]{4,3,0,2,1:T(8,128)(2,1)S(1)}, bf16[1,1,1,8,512]{4,3,0,2,1:T(8,128)(2,1)S(1)}, u32[]{:S(2)}, u32[]{:S(2)}) collective-permute-start(bf16[1,1,1,8,512]{4,3,0,2,1:T(8,128)(2,1)S(1)} %get-tuple-element.112), channel_id=1, source_target_pairs={{0,7},{1,8},{2,9},{3,10},{4,11},{5,12},{6,13},{7,14},{8,15},{9,0},... | collective-permute-start | bytes 24584 | tf_op jit(solution)/shard_map/ppermute | solution.py:136
  59.5 1.0 %collective-permute-start.8 = (bf16[1,1,1,8,512]{4,3,0,2,1:T(8,128)(2,1)S(1)}, bf16[1,1,1,8,512]{4,3,0,2,1:T(8,128)(2,1)S(1)}, u32[]{:S(2)}, u32[]{:S(2)}) collective-permute-start(bf16[1,1,1,8,512]{4,3,0,2,1:T(8,128)(2,1)S(1)} %get-tuple-element.110), channel_id=1, source_target_pairs={{0,9},{1,10},{2,11},{3,12},{4,13},{5,14},{6,15},{7,0},{8,1},{9,2},... | collective-permute-start | bytes 24584 | tf_op jit(solution)/shard_map/ppermute | solution.py:136
  60.4 1.6 %collective-permute-start.9 = (bf16[1,1,1,8,512]{4,3,0,2,1:T(8,128)(2,1)S(1)}, bf16[1,1,1,8,512]{4,3,0,2,1:T(8,128)(2,1)S(1)}, u32[]{:S(2)}, u32[]{:S(2)}) collective-permute-start(bf16[1,1,1,8,512]{4,3,0,2,1:T(8,128)(2,1)S(1)} %get-tuple-element.109), channel_id=1, source_target_pairs={{0,10},{1,11},{2,12},{3,13},{4,14},{5,15},{6,0},{7,1},{8,2},{9,3},... | collective-permute-start | bytes 24584 | tf_op jit(solution)/shard_map/ppermute | solution.py:136
  62.0 2.7 %collective-permute-start.10 = (bf16[1,1,1,8,512]{4,3,0,2,1:T(8,128)(2,1)S(1)}, bf16[1,1,1,8,512]{4,3,0,2,1:T(8,128)(2,1)S(1)}, u32[]{:S(2)}, u32[]{:S(2)}) collective-permute-start(bf16[1,1,1,8,512]{4,3,0,2,1:T(8,128)(2,1)S(1)} %get-tuple-element.108), channel_id=1, source_target_pairs={{0,11},{1,12},{2,13},{3,14},{4,15},{5,0},{6,1},{7,2},{8,3},{9,4},{... | collective-permute-start | bytes 24584 | tf_op jit(solution)/shard_map/ppermute | solution.py:136
  64.7 1.1 %collective-permute-start.11 = (bf16[1,1,1,8,512]{4,3,0,2,1:T(8,128)(2,1)S(1)}, bf16[1,1,1,8,512]{4,3,0,2,1:T(8,128)(2,1)S(1)}, u32[]{:S(2)}, u32[]{:S(2)}) collective-permute-start(bf16[1,1,1,8,512]{4,3,0,2,1:T(8,128)(2,1)S(1)} %get-tuple-element.107), channel_id=1, source_target_pairs={{0,12},{1,13},{2,14},{3,15},{4,0},{5,1},{6,2},{7,3},{8,4},{9,5},{1... | collective-permute-start | bytes 24584 | tf_op jit(solution)/shard_map/ppermute | solution.py:136
  65.8 1.0 %collective-permute-start.13 = (bf16[1,1,1,8,512]{4,3,0,2,1:T(8,128)(2,1)S(1)}, bf16[1,1,1,8,512]{4,3,0,2,1:T(8,128)(2,1)S(1)}, u32[]{:S(2)}, u32[]{:S(2)}) collective-permute-start(bf16[1,1,1,8,512]{4,3,0,2,1:T(8,128)(2,1)S(1)} %get-tuple-element.105), channel_id=1, source_target_pairs={{0,14},{1,15},{2,0},{3,1},{4,2},{5,3},{6,4},{7,5},{8,6},{9,7},{10,... | collective-permute-start | bytes 24584 | tf_op jit(solution)/shard_map/ppermute | solution.py:136
  66.8 2.6 %collective-permute-start.14 = (bf16[1,1,1,8,512]{4,3,0,2,1:T(8,128)(2,1)S(1)}, bf16[1,1,1,8,512]{4,3,0,2,1:T(8,128)(2,1)S(1)}, u32[]{:S(2)}, u32[]{:S(2)}) collective-permute-start(bf16[1,1,1,8,512]{4,3,0,2,1:T(8,128)(2,1)S(1)} %get-tuple-element.104), channel_id=1, source_target_pairs={{0,15},{1,0},{2,1},{3,2},{4,3},{5,4},{6,5},{7,6},{8,7},{9,8},{10,9... | collective-permute-start | bytes 24584 | tf_op jit(solution)/shard_map/ppermute | solution.py:136
  69.4 1.8 %collective-permute-done.12 = bf16[1,1,1,8,512]{4,3,0,2,1:T(8,128)(2,1)S(1)} collective-permute-done((bf16[1,1,1,8,512]{4,3,0,2,1:T(8,128)(2,1)S(1)}, bf16[1,1,1,8,512]{4,3,0,2,1:T(8,128)(2,1)S(1)}, u32[]{:S(2)}, u32[]{:S(2)}) %collective-permute-start.12) | collective-permute-done | bytes 8224 | tf_op jit(solution)/shard_map/ppermute | solution.py:136
  72.0 0.8 %add_add_fusion = f32[32,4,512]{2,1,0:T(4,128)} fusion(f32[32,4,512]{2,1,0:T(4,128)S(1)} %reshape.101, f32[32,4,512]{2,1,0:T(4,128)S(1)} %reshape.102, f32[512]{0:T(512)S(1)} %add.403), kind=kLoop, calls=%fused_computation.45 | loop fusion | flops 131072 | bytes 788480 | tf_op jit(solution)/shard_map/add | solution.py:145
  (135 shorter events, 9.2 us)
Async XLA Ops:
  0.6 48.5 %copy-start = (bf16[384,384]{1,0:T(8,128)(2,1)S(1)}, bf16[384,384]{1,0:T(8,128)(2,1)}, u32[]{:S(2)}) copy-start(bf16[384,384]{1,0:T(8,128)(2,1)} %param.29) | copy-start | bytes 884740
  0.7 1.4 %copy-start.1 = (bf16[128,1024]{1,0:T(8,128)(2,1)S(1)}, bf16[128,1024]{1,0:T(8,128)(2,1)}, u32[]{:S(2)}) copy-start(bf16[128,1024]{1,0:T(8,128)(2,1)} %get-tuple-element.232) | copy-start | bytes 786436 | tf_op jit(solution)/shard_map/while
  9.4 3.8 %copy-start.5 = (f32[32,384]{1,0:T(8,128)S(1)}, f32[32,384]{1,0:T(8,128)}, u32[]{:S(2)}) copy-start(f32[32,384]{1,0:T(8,128)} %param.18) | copy-start | bytes 147460
  9.4 3.8 %copy-start.6 = (f32[32,384]{1,0:T(8,128)S(1)}, f32[32,384]{1,0:T(8,128)}, u32[]{:S(2)}) copy-start(f32[32,384]{1,0:T(8,128)} %param.26) | copy-start | bytes 147460
  9.4 3.8 %copy-start.11 = (s32[32]{0:T(128)S(1)}, s32[32]{0:T(128)}, u32[]{:S(2)}) copy-start(s32[32]{0:T(128)} %param.19) | copy-start | bytes 388
  9.4 4.3 %copy-start.9 = (f32[384]{0:T(512)S(1)}, f32[384]{0:T(512)}, u32[]{:S(2)}) copy-start(f32[384]{0:T(512)} %param.27) | copy-start | bytes 4612
  9.4 4.4 %copy-start.2 = (bf16[384,1536]{1,0:T(8,128)(2,1)S(1)}, bf16[384,1536]{1,0:T(8,128)(2,1)}, u32[]{:S(2)}) copy-start(bf16[384,1536]{1,0:T(8,128)(2,1)} %param.28) | copy-start | bytes 3538948
  9.8 40.4 %collective-permute-start = (bf16[1,1,1,8,512]{4,3,0,2,1:T(8,128)(2,1)S(1)}, bf16[1,1,1,8,512]{4,3,0,2,1:T(8,128)(2,1)S(1)}, u32[]{:S(2)}, u32[]{:S(2)}) collective-permute-start(bf16[1,1,1,8,512]{4,3,0,2,1:T(8,128)(2,1)S(1)} %constant_dynamic-slice_fusion.15), channel_id=1, source_target_pairs={{0,1},{1,2},{2,3},{3,4},{4,5},{5,6},{6,7},{7,8},{8,9},{9,10},{10,1... | collective-permute-start | bytes 24584 | tf_op jit(solution)/shard_map/ppermute | solution.py:136
  13.8 6.3 %copy-start.10 = (s32[4,4,1]{1,2,0:T(1,128)S(1)}, s32[4,4,1]{1,2,0:T(1,128)}, u32[]{:S(2)}) copy-start(s32[4,4,1]{1,2,0:T(1,128)} %param.20) | copy-start | bytes 196
  49.1 2.1 %copy-start.12 = (f32[64]{0:T(128)S(1)}, f32[64]{0:T(128)}, u32[]{:S(2)}) copy-start(f32[64]{0:T(128)} %param.31) | copy-start | bytes 772
  50.3 5.7 %collective-permute-start.1 = (bf16[1,1,1,8,512]{4,3,0,2,1:T(8,128)(2,1)S(1)}, bf16[1,1,1,8,512]{4,3,0,2,1:T(8,128)(2,1)S(1)}, u32[]{:S(2)}, u32[]{:S(2)}) collective-permute-start(bf16[1,1,1,8,512]{4,3,0,2,1:T(8,128)(2,1)S(1)} %get-tuple-element.117), channel_id=1, source_target_pairs={{0,2},{1,3},{2,4},{3,5},{4,6},{5,7},{6,8},{7,9},{8,10},{9,11},{10,... | collective-permute-start | bytes 24584 | tf_op jit(solution)/shard_map/ppermute | solution.py:136
  51.3 7.6 %collective-permute-start.2 = (bf16[1,1,1,8,512]{4,3,0,2,1:T(8,128)(2,1)S(1)}, bf16[1,1,1,8,512]{4,3,0,2,1:T(8,128)(2,1)S(1)}, u32[]{:S(2)}, u32[]{:S(2)}) collective-permute-start(bf16[1,1,1,8,512]{4,3,0,2,1:T(8,128)(2,1)S(1)} %get-tuple-element.116), channel_id=1, source_target_pairs={{0,3},{1,4},{2,5},{3,6},{4,7},{5,8},{6,9},{7,10},{8,11},{9,12},{10... | collective-permute-start | bytes 24584 | tf_op jit(solution)/shard_map/ppermute | solution.py:136
  52.8 6.7 %collective-permute-start.3 = (bf16[1,1,1,8,512]{4,3,0,2,1:T(8,128)(2,1)S(1)}, bf16[1,1,1,8,512]{4,3,0,2,1:T(8,128)(2,1)S(1)}, u32[]{:S(2)}, u32[]{:S(2)}) collective-permute-start(bf16[1,1,1,8,512]{4,3,0,2,1:T(8,128)(2,1)S(1)} %get-tuple-element.115), channel_id=1, source_target_pairs={{0,4},{1,5},{2,6},{3,7},{4,8},{5,9},{6,10},{7,11},{8,12},{9,13},{1... | collective-permute-start | bytes 24584 | tf_op jit(solution)/shard_map/ppermute | solution.py:136
  53.8 6.6 %collective-permute-start.4 = (bf16[1,1,1,8,512]{4,3,0,2,1:T(8,128)(2,1)S(1)}, bf16[1,1,1,8,512]{4,3,0,2,1:T(8,128)(2,1)S(1)}, u32[]{:S(2)}, u32[]{:S(2)}) collective-permute-start(bf16[1,1,1,8,512]{4,3,0,2,1:T(8,128)(2,1)S(1)} %get-tuple-element.114), channel_id=1, source_target_pairs={{0,5},{1,6},{2,7},{3,8},{4,9},{5,10},{6,11},{7,12},{8,13},{9,14},{... | collective-permute-start | bytes 24584 | tf_op jit(solution)/shard_map/ppermute | solution.py:136
  54.4 7.6 %collective-permute-start.5 = (bf16[1,1,1,8,512]{4,3,0,2,1:T(8,128)(2,1)S(1)}, bf16[1,1,1,8,512]{4,3,0,2,1:T(8,128)(2,1)S(1)}, u32[]{:S(2)}, u32[]{:S(2)}) collective-permute-start(bf16[1,1,1,8,512]{4,3,0,2,1:T(8,128)(2,1)S(1)} %get-tuple-element.113), channel_id=1, source_target_pairs={{0,6},{1,7},{2,8},{3,9},{4,10},{5,11},{6,12},{7,13},{8,14},{9,15},... | collective-permute-start | bytes 24584 | tf_op jit(solution)/shard_map/ppermute | solution.py:136
  56.0 8.7 %collective-permute-start.6 = (bf16[1,1,1,8,512]{4,3,0,2,1:T(8,128)(2,1)S(1)}, bf16[1,1,1,8,512]{4,3,0,2,1:T(8,128)(2,1)S(1)}, u32[]{:S(2)}, u32[]{:S(2)}) collective-permute-start(bf16[1,1,1,8,512]{4,3,0,2,1:T(8,128)(2,1)S(1)} %get-tuple-element.112), channel_id=1, source_target_pairs={{0,7},{1,8},{2,9},{3,10},{4,11},{5,12},{6,13},{7,14},{8,15},{9,0},... | collective-permute-start | bytes 24584 | tf_op jit(solution)/shard_map/ppermute | solution.py:136
  58.9 6.9 %collective-permute-start.7 = (bf16[1,1,1,8,512]{4,3,0,2,1:T(8,128)(2,1)S(1)}, bf16[1,1,1,8,512]{4,3,0,2,1:T(8,128)(2,1)S(1)}, u32[]{:S(2)}, u32[]{:S(2)}) collective-permute-start(bf16[1,1,1,8,512]{4,3,0,2,1:T(8,128)(2,1)S(1)} %get-tuple-element.111), channel_id=1, source_target_pairs={{0,8},{1,9},{2,10},{3,11},{4,12},{5,13},{6,14},{7,15},{8,0},{9,1},... | collective-permute-start | bytes 24584 | tf_op jit(solution)/shard_map/ppermute | solution.py:136
  59.5 6.3 %collective-permute-start.8 = (bf16[1,1,1,8,512]{4,3,0,2,1:T(8,128)(2,1)S(1)}, bf16[1,1,1,8,512]{4,3,0,2,1:T(8,128)(2,1)S(1)}, u32[]{:S(2)}, u32[]{:S(2)}) collective-permute-start(bf16[1,1,1,8,512]{4,3,0,2,1:T(8,128)(2,1)S(1)} %get-tuple-element.110), channel_id=1, source_target_pairs={{0,9},{1,10},{2,11},{3,12},{4,13},{5,14},{6,15},{7,0},{8,1},{9,2},... | collective-permute-start | bytes 24584 | tf_op jit(solution)/shard_map/ppermute | solution.py:136
  60.4 6.4 %collective-permute-start.9 = (bf16[1,1,1,8,512]{4,3,0,2,1:T(8,128)(2,1)S(1)}, bf16[1,1,1,8,512]{4,3,0,2,1:T(8,128)(2,1)S(1)}, u32[]{:S(2)}, u32[]{:S(2)}) collective-permute-start(bf16[1,1,1,8,512]{4,3,0,2,1:T(8,128)(2,1)S(1)} %get-tuple-element.109), channel_id=1, source_target_pairs={{0,10},{1,11},{2,12},{3,13},{4,14},{5,15},{6,0},{7,1},{8,2},{9,3},... | collective-permute-start | bytes 24584 | tf_op jit(solution)/shard_map/ppermute | solution.py:136
  62.0 7.4 %collective-permute-start.10 = (bf16[1,1,1,8,512]{4,3,0,2,1:T(8,128)(2,1)S(1)}, bf16[1,1,1,8,512]{4,3,0,2,1:T(8,128)(2,1)S(1)}, u32[]{:S(2)}, u32[]{:S(2)}) collective-permute-start(bf16[1,1,1,8,512]{4,3,0,2,1:T(8,128)(2,1)S(1)} %get-tuple-element.108), channel_id=1, source_target_pairs={{0,11},{1,12},{2,13},{3,14},{4,15},{5,0},{6,1},{7,2},{8,3},{9,4},{... | collective-permute-start | bytes 24584 | tf_op jit(solution)/shard_map/ppermute | solution.py:136
  64.7 4.7 %collective-permute-start.11 = (bf16[1,1,1,8,512]{4,3,0,2,1:T(8,128)(2,1)S(1)}, bf16[1,1,1,8,512]{4,3,0,2,1:T(8,128)(2,1)S(1)}, u32[]{:S(2)}, u32[]{:S(2)}) collective-permute-start(bf16[1,1,1,8,512]{4,3,0,2,1:T(8,128)(2,1)S(1)} %get-tuple-element.107), channel_id=1, source_target_pairs={{0,12},{1,13},{2,14},{3,15},{4,0},{5,1},{6,2},{7,3},{8,4},{9,5},{1... | collective-permute-start | bytes 24584 | tf_op jit(solution)/shard_map/ppermute | solution.py:136
  65.8 5.5 %collective-permute-start.12 = (bf16[1,1,1,8,512]{4,3,0,2,1:T(8,128)(2,1)S(1)}, bf16[1,1,1,8,512]{4,3,0,2,1:T(8,128)(2,1)S(1)}, u32[]{:S(2)}, u32[]{:S(2)}) collective-permute-start(bf16[1,1,1,8,512]{4,3,0,2,1:T(8,128)(2,1)S(1)} %get-tuple-element.106), channel_id=1, source_target_pairs={{0,13},{1,14},{2,15},{3,0},{4,1},{5,2},{6,3},{7,4},{8,5},{9,6},{10... | collective-permute-start | bytes 24584 | tf_op jit(solution)/shard_map/ppermute | solution.py:136
  65.8 5.4 %collective-permute-start.13 = (bf16[1,1,1,8,512]{4,3,0,2,1:T(8,128)(2,1)S(1)}, bf16[1,1,1,8,512]{4,3,0,2,1:T(8,128)(2,1)S(1)}, u32[]{:S(2)}, u32[]{:S(2)}) collective-permute-start(bf16[1,1,1,8,512]{4,3,0,2,1:T(8,128)(2,1)S(1)} %get-tuple-element.105), channel_id=1, source_target_pairs={{0,14},{1,15},{2,0},{3,1},{4,2},{5,3},{6,4},{7,5},{8,6},{9,7},{10,... | collective-permute-start | bytes 24584 | tf_op jit(solution)/shard_map/ppermute | solution.py:136
  66.8 4.7 %collective-permute-start.14 = (bf16[1,1,1,8,512]{4,3,0,2,1:T(8,128)(2,1)S(1)}, bf16[1,1,1,8,512]{4,3,0,2,1:T(8,128)(2,1)S(1)}, u32[]{:S(2)}, u32[]{:S(2)}) collective-permute-start(bf16[1,1,1,8,512]{4,3,0,2,1:T(8,128)(2,1)S(1)} %get-tuple-element.104), channel_id=1, source_target_pairs={{0,15},{1,0},{2,1},{3,2},{4,3},{5,4},{6,5},{7,6},{8,7},{9,8},{10,9... | collective-permute-start | bytes 24584 | tf_op jit(solution)/shard_map/ppermute | solution.py:136
  (11 other events, 12.5 us)
